TPU v7x, 32 devices: a whole 2x2x4 slice. The times are simulated.
32 devices in a mesh: tok: 4 (over z), hid: 8 (over y, x, core).
Axes of the slice: x: 2, y: 2, z: 4, core: 2. Of those that a mesh axis runs over, the one named last changes fastest.
Arguments:
- tokens: bfloat16 [4096, 8192], P('tok', 'hid'), may hold values from -6 to 6
- qkv_weight: bfloat16 [8192, 10240], P('tok', 'hid'), may hold values from -0.09375 to 0.09375
- qkv_cotangent: bfloat16 [4096, 10240], P('tok', 'hid'), may hold values from -6 to 6
Outputs:
- projected: bfloat16 [4096, 10240], P('tok', 'hid')
- input_grad: bfloat16 [4096, 8192], P('tok', 'hid')
- weight_grad: bfloat16 [8192, 10240], P('tok', 'hid')
All inputs are finite; a program needn't handle non-finite values.
Results may differ from a plain program's by a relative error of at most 0.012.
Values may be sent and summed in bfloat16 or wider, within the bound.
A program may use at most 192 MiB of HBM per device.

v0:
```python
import jax
import jax.numpy as jnp
from jax import lax
from jax.sharding import PartitionSpec as P


def local(tokens, qkv_weight, qkv_cotangent):
    local_rows = tokens.shape[0]
    full_rows = lax.all_gather(tokens, "hid", axis=1, tiled=True)
    segment = lax.all_gather(qkv_weight, "tok", axis=0, tiled=True)
    features = full_rows
    summed = jnp.dot(features, segment, preferred_element_type=jnp.float32)
    backward = lax.dot_general(
        qkv_cotangent, segment, (((1,), (1,)), ((), ())), preferred_element_type=jnp.float32
    )
    partial_grad = backward.astype(jnp.bfloat16)
    summed, partial_grad = (summed, partial_grad)
    projected = summed.astype(jnp.bfloat16)
    input_grad = (
        lax.psum_scatter(partial_grad, "hid", scatter_dimension=1, tiled=True)
        .astype(jnp.float32)
        .astype(jnp.bfloat16)
    )
    factor = float(local_rows * lax.axis_size("tok")) ** (-0.5)
    features = full_rows
    grad_block = lax.psum_scatter(
        lax.dot_general(
            features, qkv_cotangent, (((0,), (0,)), ((), ())), preferred_element_type=jnp.float32
        ).astype(jnp.bfloat16),
        "tok",
        scatter_dimension=0,
        tiled=True,
    ).astype(jnp.float32)
    weight_grad = (grad_block * factor).astype(jnp.bfloat16)
    return (projected, input_grad, weight_grad)


def solution(mesh):
    in_specs = (P("tok", "hid"), P("tok", "hid"), P("tok", "hid"))
    out_specs = (P("tok", "hid"), P("tok", "hid"), P("tok", "hid"))
    return jax.shard_map(local, mesh=mesh, in_specs=in_specs, out_specs=out_specs, check_vma=False)
```

profile of v0, /device:TPU:0, one launch (start us, length us, event | category | flops | bytes accessed | tf_op | source)
XLA Modules:
  0.0 937.1 jit_solution(6630098638862187927)
XLA Ops:
  7.2 0.0 copy-start
  7.2 0.0 all-gather.3.cloned.1.call-start
  7.2 0.7 all-gather.3.cloned.1.call-update
  7.9 0.0 all-gather.5.cloned.1.call-start
  8.0 0.7 all-gather.5.cloned.1.call-update
  8.7 0.0 reduce-scatter.5.cloned.1.call-start
  8.7 93.7 %all-gather.3.cloned.1.call-done = bf16[1024,8192]{1,0:T(8,128)(2,1)} async-done(((bf16[1024,1024]{1,0:T(8,128)(2,1)}), bf16[1024,8192]{1,0:T(8,128)(2,1)}) %all-gather.3.cloned.1.call-update) | async-done | bytes 16777232 | tf_op jit(solution)/shard_map/all_gather | solution.py:9
  102.4 0.0 copy-done
  102.4 31.9 %convolution_convert_fusion = bf16[8192,1280]{1,0:T(8,128)(2,1)} fusion(bf16[1024,8192]{1,0:T(8,128)(2,1)} %all-gather.3.cloned.1.call-done, bf16[1024,1280]{1,0:T(8,128)(2,1)S(1)} %copy-done), kind=kOutput, calls=%fused_computation | convolution fusion | flops 21485322240 | bytes 40370176 | tf_op jit(solution)/shard_map/dot_general | solution.py:27
  134.2 0.0 reduce-scatter.5.cloned.1.call-update
  134.3 0.2 reduce-scatter.3.cloned.1.call-start
  134.5 326.3 %all-gather.5.cloned.1.call-done = bf16[8192,1280]{1,0:T(8,128)(2,1)} async-done(((bf16[2048,1280]{1,0:T(8,128)(2,1)}), bf16[8192,1280]{1,0:T(8,128)(2,1)}) %all-gather.5.cloned.1.call-update) | async-done | bytes 20971536 | tf_op jit(solution)/shard_map/all_gather | solution.py:10
  460.8 27.2 %convolution_convert_fusion.1 = bf16[1024,8192]{1,0:T(8,128)(2,1)} fusion(bf16[1024,1280]{1,0:T(8,128)(2,1)S(1)} %copy-done, bf16[8192,1280]{1,0:T(8,128)(2,1)} %all-gather.5.cloned.1.call-done), kind=kOutput, calls=%fused_computation.1 | convolution fusion | flops 21483225088 | bytes 40370176 | tf_op jit(solution)/shard_map/dot_general | solution.py:13
  488.0 0.0 reduce-scatter.3.cloned.1.call-update
  488.0 0.0 copy-start.1
  488.0 28.1 %convolution_convert_fusion.2 = bf16[1024,1280]{1,0:T(8,128)(2,1)} fusion(bf16[1024,8192]{1,0:T(8,128)(2,1)} %all-gather.3.cloned.1.call-done, bf16[8192,1280]{1,0:T(8,128)(2,1)} %all-gather.5.cloned.1.call-done), kind=kOutput, calls=%fused_computation.3 | convolution fusion | flops 21476147200 | bytes 40370176 | tf_op jit(solution)/shard_map/dot_general | solution.py:12
  516.1 293.1 %reduce-scatter.5.cloned.1.call-done = bf16[2048,1280]{1,0:T(8,128)(2,1)} async-done(((bf16[8192,1280]{1,0:T(8,128)(2,1)}), bf16[2048,1280]{1,0:T(8,128)(2,1)}) %reduce-scatter.5.cloned.1.call-update) | async-done | bytes 5242896 | tf_op jit(solution)/shard_map/reduce_scatter | solution.py:26
  809.2 5.8 multiply_convert_fusion
  815.0 115.5 %reduce-scatter.3.cloned.1.call-done = bf16[1024,1024]{1,0:T(8,128)(2,1)} async-done(((bf16[1024,8192]{1,0:T(8,128)(2,1)}), bf16[1024,1024]{1,0:T(8,128)(2,1)}) %reduce-scatter.3.cloned.1.call-update) | async-done | bytes 2097168 | tf_op jit(solution)/shard_map/reduce_scatter | solution.py:20
  930.5 0.0 copy-done.1
Async XLA Ops:
  7.2 95.2 %copy-start = (bf16[1024,1280]{1,0:T(8,128)(2,1)S(1)}, bf16[1024,1280]{1,0:T(8,128)(2,1)}, u32[]{:S(2)}) copy-start(bf16[1024,1280]{1,0:T(8,128)(2,1)} %param.5) | copy-start | bytes 7864324
  7.2 95.2 %all-gather.3.cloned.1.call-start = ((), (), s32[]{:S(2)}) async-start(), calls=%async_computation.2 | async-start | bytes 18874368 | tf_op jit(solution)/shard_map/all_gather | solution.py:9
  7.9 452.9 %all-gather.5.cloned.1.call-start = ((), (), s32[]{:S(2)}) async-start(), calls=%async_computation.3 | async-start | bytes 26214400 | tf_op jit(solution)/shard_map/all_gather | solution.py:10
  8.7 800.5 %reduce-scatter.5.cloned.1.call-start = ((), (), s32[]{:S(2)}) async-start(), calls=%async_computation.5 | async-start | bytes 26214400 | tf_op jit(solution)/shard_map/reduce_scatter | solution.py:26
  134.3 796.2 %reduce-scatter.3.cloned.1.call-start = ((), (), s32[]{:S(2)}) async-start(), calls=%async_computation.4 | async-start | bytes 18874368 | tf_op jit(solution)/shard_map/reduce_scatter | solution.py:20
  488.0 442.5 %copy-start.1 = (bf16[1024,1280]{1,0:T(8,128)(2,1)S(1)}, bf16[1024,1280]{1,0:T(8,128)(2,1)}, u32[]{:S(2)}) copy-start(bf16[1024,1280]{1,0:T(8,128)(2,1)} %param.5) | copy-start | bytes 7864324
Sparse Core Ops, SparseCore 0:
  9.9 92.4 all-gather.2
  104.0 356.8 all-gather.4
  463.2 345.9 reduce-scatter.4
  813.1 117.3 reduce-scatter.2
where the time goes:
time: 937 us
  waiting for transfers between devices  830 us (89%)
  matrix products  87.1 us (9%)
  between operations  13.8 us (1%)
    all_gather x1, waiting for transfers between devices, local(): segment = lax.all_gather(qkv_weight, 'tok', axis=0, tiled=True)  326 us
    reduce_scatter x1, waiting for transfers between devices, local(): lax.psum_scatter(lax.dot_general(features, qkv_cotangent, (((0,), (0,)),...  293 us
    reduce_scatter x1, waiting for transfers between devices, local(): lax.psum_scatter(partial_grad, 'hid', scatter_dimension=1, tiled=True)  116 us
    all_gather x1, waiting for transfers between devices, local(): full_rows = lax.all_gather(tokens, 'hid', axis=1, tiled=True)  93.7 us
    dot_general x1, matrix products, local(): lax.dot_general(features, qkv_cotangent, (((0,), (0,)), ((), ())), prefer...  31.9 us
    dot_general x1, matrix products, local(): summed = jnp.dot(features, segment, preferred_element_type=jnp.float32)  28.1 us
    dot_general x1, matrix products, local(): lax.dot_general(qkv_cotangent, segment, (((1,), (1,)), ((), ())), preferr...  27.2 us
  transfers between devices with their start and end apart: 4, of which 4 were waited for; matrix products, arithmetic and copies ran while one was open for 10% of the time, Pallas kernels for 0%

commit v1 on v0

--- a/solution.py
+++ b/solution.py
@@ -4,10 +4,18 @@
 from jax.sharding import PartitionSpec as P
 
 
+def switch_point_here(x_part, device_axis):
+    value_now = lax.axis_size(device_axis)
+    k_now = jnp.stack(value_now * [x_part], axis=0)
+    wide_out = lax.all_to_all(k_now, device_axis, split_axis=0, concat_axis=0)
+    res = jnp.concatenate(wide_out, axis=0)
+    return res
+
+
 def local(tokens, qkv_weight, qkv_cotangent):
     local_rows = tokens.shape[0]
     full_rows = lax.all_gather(tokens, "hid", axis=1, tiled=True)
-    segment = lax.all_gather(qkv_weight, "tok", axis=0, tiled=True)
+    segment = switch_point_here(qkv_weight, "tok")
     features = full_rows
     summed = jnp.dot(features, segment, preferred_element_type=jnp.float32)
     backward = lax.dot_general(

time: 937 us -> 1080 us (1.15)
  blocking collectives: 0 us -> 791 us
  waiting for transfers between devices: 830 us -> 176 us
    all_to_all x0 -> x1, blocking collectives: none -> 791 us  [switch_point_here(): wide_out = lax.all_to_all(k_now, device_axis, split_axis=0, concat_axis=0)]
    all_gather x1 -> x0, waiting for transfers between devices: 326 us -> none  [local(): segment = lax.all_gather(qkv_weight, 'tok', axis=0, tiled=True)]
    reduce_scatter x1, waiting for transfers between devices: 293 us -> 0.01 us  [local(): lax.psum_scatter(lax.dot_general(features, qkv_cotangent, (((0,), (0,)),...]
    reduce_scatter x1, waiting for transfers between devices: 116 us -> 81.3 us  [local(): lax.psum_scatter(partial_grad, 'hid', scatter_dimension=1, tiled=True)]
  transfers between devices with their start and end apart: 4 -> 3, of which waited for: 4 -> 2; matrix products, arithmetic and copies ran while one was open for 10% -> 6% of each run, Pallas kernels for 0% -> 0%
where the time goes in v1:
time: 1080 us
  blocking collectives  791 us (73%)
  waiting for transfers between devices  176 us (16%)
  matrix products  87 us (8%)
  between operations  13.8 us (1%)
    all_to_all x1, blocking collectives, switch_point_here(): wide_out = lax.all_to_all(k_now, device_axis, split_axis=0, concat_axis=0)  791 us
    all_gather x1, waiting for transfers between devices, local(): full_rows = lax.all_gather(tokens, 'hid', axis=1, tiled=True)  94.4 us
    reduce_scatter x1, waiting for transfers between devices, local(): lax.psum_scatter(partial_grad, 'hid', scatter_dimension=1, tiled=True)  81.3 us
    dot_general x1, matrix products, local(): lax.dot_general(features, qkv_cotangent, (((0,), (0,)), ((), ())), prefer...  32 us
    dot_general x1, matrix products, local(): summed = jnp.dot(features, segment, preferred_element_type=jnp.float32)  28.1 us
    dot_general x1, matrix products, local(): lax.dot_general(qkv_cotangent, segment, (((1,), (1,)), ((), ())), preferr...  26.9 us
  transfers between devices with their start and end apart: 3, of which 2 were waited for; matrix products, arithmetic and copies ran while one was open for 6% of the time, Pallas kernels for 0%

profile of v1, /device:TPU:0, one launch (start us, length us, event | category | flops | bytes accessed | tf_op | source)
XLA Modules:
  0.0 1078.7 jit_solution(16915964440779842357)
XLA Ops:
  7.2 0.0 copy-start
  7.2 0.0 all-gather.2.cloned.1.call-start
  7.2 0.7 all-gather.2.cloned.1.call-update
  7.9 0.0 reduce-scatter.5.cloned.1.call-start
  8.0 94.4 %all-gather.2.cloned.1.call-done = bf16[1024,8192]{1,0:T(8,128)(2,1)} async-done(((bf16[1024,1024]{1,0:T(8,128)(2,1)}), bf16[1024,8192]{1,0:T(8,128)(2,1)}) %all-gather.2.cloned.1.call-update) | async-done | bytes 16777232 | tf_op jit(solution)/shard_map/all_gather | solution.py:17
  102.4 0.0 copy-done
  102.4 32.0 %convolution_convert_fusion = bf16[8192,1280]{1,0:T(8,128)(2,1)} fusion(bf16[1024,8192]{1,0:T(8,128)(2,1)} %all-gather.2.cloned.1.call-done, bf16[1024,1280]{1,0:T(8,128)(2,1)S(1)} %copy-done), kind=kOutput, calls=%fused_computation | convolution fusion | flops 21485322240 | bytes 40370176 | tf_op jit(solution)/shard_map/dot_general | solution.py:35
  134.4 0.0 reduce-scatter.5.cloned.1.call-update
  134.4 0.0 reduce-scatter.3.cloned.1.call-start
  134.5 5.0 stack.2
  139.4 790.6 %all_to_all.5 = bf16[4,2048,1280]{2,1,0:T(8,128)(2,1)} all-to-all(bf16[4,2048,1280]{2,1,0:T(8,128)(2,1)S(1)} %stack.2), channel_id=1, replica_groups=mesh['tok'=4,'hid'=8] {'tok'}, dimensions={0} | all-to-all | bytes 41943040 | tf_op jit(solution)/shard_map/all_to_all | solution.py:10
  930.0 26.9 %convolution_convert_fusion.1 = bf16[1024,8192]{1,0:T(8,128)(2,1)} fusion(bf16[1024,1280]{1,0:T(8,128)(2,1)S(1)} %copy-done, bf16[8192,1280]{1,0:T(8,128)(2,1)} %bitcast.7), kind=kOutput, calls=%fused_computation.1 | convolution fusion | flops 21483225088 | bytes 40370176 | tf_op jit(solution)/shard_map/dot_general | solution.py:21
  956.9 0.0 reduce-scatter.3.cloned.1.call-update
  957.0 0.0 copy-start.1
  957.0 28.1 %convolution_convert_fusion.2 = bf16[1024,1280]{1,0:T(8,128)(2,1)} fusion(bf16[1024,8192]{1,0:T(8,128)(2,1)} %all-gather.2.cloned.1.call-done, bf16[8192,1280]{1,0:T(8,128)(2,1)} %bitcast.8), kind=kOutput, calls=%fused_computation.3 | convolution fusion | flops 21476147200 | bytes 40370176 | tf_op jit(solution)/shard_map/dot_general | solution.py:20
  985.0 0.0 reduce-scatter.5.cloned.1.call-done
  985.0 5.8 multiply_convert_fusion
  990.9 81.3 %reduce-scatter.3.cloned.1.call-done = bf16[1024,1024]{1,0:T(8,128)(2,1)} async-done(((bf16[1024,8192]{1,0:T(8,128)(2,1)}), bf16[1024,1024]{1,0:T(8,128)(2,1)}) %reduce-scatter.3.cloned.1.call-update) | async-done | bytes 2097168 | tf_op jit(solution)/shard_map/reduce_scatter | solution.py:28
  1072.1 0.0 copy-done.1
Async XLA Ops:
  7.2 95.2 %copy-start = (bf16[1024,1280]{1,0:T(8,128)(2,1)S(1)}, bf16[1024,1280]{1,0:T(8,128)(2,1)}, u32[]{:S(2)}) copy-start(bf16[1024,1280]{1,0:T(8,128)(2,1)} %param.5) | copy-start | bytes 7864324
  7.2 95.2 %all-gather.2.cloned.1.call-start = ((), (), s32[]{:S(2)}) async-start(), calls=%async_computation.3 | async-start | bytes 18874368 | tf_op jit(solution)/shard_map/all_gather | solution.py:17
  7.9 977.1 %reduce-scatter.5.cloned.1.call-start = ((), (), s32[]{:S(2)}) async-start(), calls=%async_computation.5 | async-start | bytes 26214400 | tf_op jit(solution)/shard_map/reduce_scatter | solution.py:34
  134.4 937.7 %reduce-scatter.3.cloned.1.call-start = ((), (), s32[]{:S(2)}) async-start(), calls=%async_computation.4 | async-start | bytes 18874368 | tf_op jit(solution)/shard_map/reduce_scatter | solution.py:28
  957.0 115.2 %copy-start.1 = (bf16[1024,1280]{1,0:T(8,128)(2,1)S(1)}, bf16[1024,1280]{1,0:T(8,128)(2,1)}, u32[]{:S(2)}) copy-start(bf16[1024,1280]{1,0:T(8,128)(2,1)} %param.5) | copy-start | bytes 7864324
Sparse Core Ops, SparseCore 0:
  9.9 92.4 all-gather.1
  134.5 717.3 reduce-scatter.4
  957.1 115.0 reduce-scatter.2
